TPU v7x, 32 devices: a whole 2x2x4 slice. The times are simulated.
32 devices in a mesh: seq: 4 (over y, core), user: 8 (over z, x).
Axes of the slice: x: 2, y: 2, z: 4, core: 2. Of those that a mesh axis runs over, the one named last changes fastest.
Arguments:
- history: bfloat16 [8, 2048, 256], P('user', 'seq'), may hold values from -6 to 6
- cotangent: bfloat16 [8, 2048, 256], P('user', 'seq'), may hold values from -6 to 6
- weights: bfloat16 [4, 3, 256, 256], replicated, may hold values from -0.21875 to 0.21875
- ln_gain: float32 [4, 256], replicated, may hold values from 0.1 to 1.9
- conv_bias: float32 [4, 256], replicated, may hold values from -3 to 3
- pooled_grad: bfloat16 [8, 64, 128], P('user', 'seq'), may hold values from -6 to 6
- table_owner: int32 [64], P('seq'), may hold values from 0 to 7, as said below
- row_ids: int32 [8, 64], P('user', 'seq'), may hold values from 0 to 999999
Outputs:
- d_history: bfloat16 [8, 2048, 256], P('user', 'seq')
- grad_weights: float32 [4, 3, 256, 256], replicated
- grad_gain: float32 [4, 256], replicated
- grad_bias: float32 [4, 256], replicated
- table_grad: float32 [64, 8, 128], P(('seq', 'user'))
Inputs may be any that keep to these rules, and one draw needn't show every extreme that they name: `table_owner`: within each block of 16 consecutive tables, every user index owns exactly 2 tables.
All inputs are finite; a program needn't handle non-finite values.
Results may differ from a plain program's by a relative error of at most 0.0095.
Values may be sent and summed in bfloat16 or wider, within the bound.
A program may use at most 64 MiB of HBM per device.

v0:
```python
import math
import jax
import jax.numpy as jnp
from jax import lax
from jax.sharding import PartitionSpec as P

TAPS = 3
LAYERS = 4
epsilon = 1e-05


def passed_along(block, axis, distance):
    devices = range(lax.axis_size(axis))
    route = [(i - distance, i) for i in devices if i - distance in devices]
    return lax.ppermute(block, axis, route)


def gelu_tanh(values):
    return jax.nn.gelu(values, approximate=True)


def gelu_slope(values, upstream):
    return jax.vjp(gelu_tanh, values)[1](upstream)[0]


def normalize(resid_field):
    center = resid_field - jnp.mean(resid_field, -1, keepdims=True)
    inverse = lax.rsqrt(jnp.mean(center * center, -1, keepdims=True) + epsilon)
    return (center * inverse, inverse)


def dilated(padded, kernel, shift_bias, dilation):
    user_count, total_len, channels = padded.shape
    out_len = total_len - (TAPS - 1) * dilation
    result = jnp.zeros((user_count * out_len, kernel.shape[2]), jnp.float32) + shift_bias
    for tap_index in range(TAPS):
        offset = (TAPS - 1 - tap_index) * dilation
        window = padded[:, offset : offset + out_len].reshape(user_count * out_len, channels)
        result = result + jnp.dot(window, kernel[tap_index], preferred_element_type=jnp.float32)
    return result.reshape(user_count, out_len, kernel.shape[2])


def coalesce(pieces):
    got_rows, got_ids = pieces
    per_owner = got_rows.shape[2]
    flat_rows = got_rows.reshape(got_rows.shape[0], per_owner, got_rows.shape[3])
    key_grid = got_ids.reshape(got_ids.shape[0], per_owner).T
    matches = (key_grid[:, :, None] == key_grid[:, None, :]).astype(jnp.bfloat16)
    return jnp.einsum("tuv,vte->tue", matches, flat_rows, preferred_element_type=jnp.float32)


def body(history, cotangent, weights, ln_gain, conv_bias, pooled_grad, table_owner, row_ids):
    user_count, length, channels = history.shape
    row_count = user_count * length
    stored = []
    resid_field = history.astype(jnp.float32)
    for layer_num in range(LAYERS):
        dilation = 2**layer_num
        lookback = (TAPS - 1) * dilation
        normed, inverse = normalize(resid_field)
        hidden = gelu_tanh(normed * ln_gain[layer_num]).astype(jnp.bfloat16)
        border = passed_along(hidden[:, length - lookback :], "seq", 1)
        padded = jnp.concatenate([border, hidden], 1)
        stored.append((resid_field, padded))
        resid_field = resid_field + dilated(
            padded, weights[layer_num], conv_bias[layer_num], dilation
        )
    grad_flow = cotangent.astype(jnp.float32)
    weight_terms = [None] * LAYERS
    gain_terms = [None] * LAYERS
    bias_terms = [None] * LAYERS
    for layer_num in reversed(range(LAYERS)):
        dilation = 2**layer_num
        lookback = (TAPS - 1) * dilation
        field_in, padded = stored[layer_num]
        flow_half = grad_flow.astype(jnp.bfloat16)
        flow_flat = flow_half.reshape(row_count, channels)
        bias_terms[layer_num] = jnp.sum(grad_flow, (0, 1))
        tap_terms = []
        for tap_index in range(TAPS):
            offset = lookback - tap_index * dilation
            window = padded[:, offset : offset + length].reshape(row_count, channels)
            tap_terms.append(
                lax.dot_general(
                    window, flow_flat, (((0,), (0,)), ((), ())), preferred_element_type=jnp.float32
                )
            )
        weight_terms[layer_num] = jnp.stack(tap_terms)
        future = passed_along(flow_half[:, :lookback], "seq", -1)
        extended = jnp.concatenate([flow_half, future], 1)
        backward = jnp.zeros((row_count, channels), jnp.float32)
        for tap_index in range(TAPS):
            offset = tap_index * dilation
            window = extended[:, offset : offset + length].reshape(row_count, channels)
            backward = backward + lax.dot_general(
                window,
                weights[layer_num, tap_index],
                (((1,), (1,)), ((), ())),
                preferred_element_type=jnp.float32,
            )
        normed, inverse = normalize(field_in)
        slopes = gelu_slope(
            normed * ln_gain[layer_num], backward.reshape(user_count, length, channels)
        )
        gain_terms[layer_num] = jnp.sum(slopes * normed, (0, 1))
        scaled = slopes * ln_gain[layer_num]
        grad_flow = grad_flow + inverse * (
            scaled
            - jnp.mean(scaled, -1, keepdims=True)
            - normed * jnp.mean(scaled * normed, -1, keepdims=True)
        )
    weight_local = jnp.stack(weight_terms)
    gain_local = jnp.stack(gain_terms)
    bias_local = jnp.stack(bias_terms)
    weight_total, gain_total, bias_total = lax.psum(
        (weight_local, gain_local, bias_local), ("seq", "user")
    )
    factor = 1.0 / math.sqrt(user_count * lax.axis_size("user") * length * lax.axis_size("seq"))
    listing = jnp.argsort(table_owner, stable=True)
    per_owner = listing.shape[0] // lax.axis_size("user")
    send_rows = jnp.take(pooled_grad, listing, axis=1).reshape(
        user_count, lax.axis_size("user"), per_owner, pooled_grad.shape[2]
    )
    send_ids = jnp.take(row_ids, listing, axis=1).reshape(
        user_count, lax.axis_size("user"), per_owner
    )
    table_grad = coalesce(
        (
            lax.all_to_all(send_rows, "user", split_axis=1, concat_axis=0, tiled=True),
            lax.all_to_all(send_ids, "user", split_axis=1, concat_axis=0, tiled=True),
        )
    )
    return (
        grad_flow.astype(jnp.bfloat16),
        weight_total * factor,
        gain_total * factor,
        bias_total * factor,
        table_grad,
    )


def solution(mesh):
    in_specs = (
        P("user", "seq", None),
        P("user", "seq", None),
        P(),
        P(),
        P(),
        P("user", "seq", None),
        P("seq"),
        P("user", "seq"),
    )
    out_specs = (P("user", "seq", None), P(), P(), P(), P(("seq", "user"), None, None))
    return jax.shard_map(body, mesh=mesh, in_specs=in_specs, out_specs=out_specs, check_vma=False)
```

profile of v0, /device:TPU:0, one launch (start us, length us, event | category | flops | bytes accessed | tf_op | source)
XLA Modules:
  0.0 236.2 jit_solution(5344520800691517173)
XLA Ops:
  7.2 0.8 fusion.190
  8.0 1.1 convert_reduce_fusion
  9.2 1.2 fusion.30
  10.3 1.3 fusion.21
  11.6 2.4 %collective-permute-start = (bf16[1,2,256]{2,1,0:T(2,128)(2,1)S(1)}, bf16[1,2,256]{2,1,0:T(2,128)(2,1)S(1)}, u32[]{:S(2)}, u32[]{:S(2)}) collective-permute-start(bf16[1,2,256]{2,1,0:T(2,128)(2,1)S(1)} %slice.220), channel_id=1, source_target_pairs={{0,8},{8,16},{16,24},{1,9},{9,17},{17,25},{2,10},{10,18},{18,26},{... | collective-permute-start | bytes 3080 | tf_op jit(solution)/shard_map/ppermute | solution.py:15
  14.0 0.7 slice.198
  14.7 1.3 collective-permute-start.3
  16.0 1.9 sort.17
  17.9 1.3 gather_fusion
  19.3 0.7 reshape.430
  19.9 6.6 %all-to-all-start = ((s32[1,8,2]{2,0,1:T(1,128)}), s32[1,8,2]{2,0,1:T(1,128)S(1)}, u32[]{:S(2)}, u32[]{:S(2)}) async-start(s32[1,8,2]{2,0,1:T(1,128)} %bitcast.75), calls=%async_computation | async-start | bytes 8192 | tf_op jit(solution)/shard_map/all_to_all | solution.py:130
  26.6 1.2 fusion.104
  27.8 1.2 convolution_add_fusion.16
  29.6 0.7 fusion.162
  30.3 0.7 constant_dynamic-update-slice_fusion.1
  31.0 2.0 all-to-all-done
  33.0 4.0 %all-to-all-start.1 = ((bf16[1,8,2,128]{3,2,0,1:T(2,128)(2,1)}), bf16[1,8,2,128]{3,2,0,1:T(2,128)(2,1)S(1)}, u32[]{:S(2)}, u32[]{:S(2)}) async-start(bf16[1,8,2,128]{3,2,0,1:T(2,128)(2,1)} %fusion.162), calls=%async_computation.1 | async-start | bytes 8192 | tf_op jit(solution)/shard_map/all_to_all | solution.py:129
  37.2 1.1 convolution_add_fusion.15
  38.3 1.3 fusion.192
  40.1 3.5 %collective-permute-start.1 = (bf16[1,4,256]{2,1,0:T(4,128)(2,1)S(1)}, bf16[1,4,256]{2,1,0:T(4,128)(2,1)S(1)}, u32[]{:S(2)}, u32[]{:S(2)}) collective-permute-start(bf16[1,4,256]{2,1,0:T(4,128)(2,1)S(1)} %slice.223), channel_id=1, source_target_pairs={{0,8},{8,16},{16,24},{1,9},{9,17},{17,25},{2,10},{10,18},{18,26},{... | collective-permute-start | bytes 6152 | tf_op jit(solution)/shard_map/ppermute | solution.py:15
  43.7 1.1 convolution_add_fusion.13
  44.8 1.1 convolution_add_fusion.12
  46.0 1.3 fusion.193
  47.8 4.5 %collective-permute-start.2 = (bf16[1,8,256]{2,1,0:T(8,128)(2,1)S(1)}, bf16[1,8,256]{2,1,0:T(8,128)(2,1)S(1)}, u32[]{:S(2)}, u32[]{:S(2)}) collective-permute-start(bf16[1,8,256]{2,1,0:T(8,128)(2,1)S(1)} %slice.226), channel_id=1, source_target_pairs={{0,8},{8,16},{16,24},{1,9},{9,17},{17,25},{2,10},{10,18},{18,26},{... | collective-permute-start | bytes 12296 | tf_op jit(solution)/shard_map/ppermute | solution.py:15
  52.3 1.1 convolution_add_fusion.10
  53.4 1.1 convolution_add_fusion.9
  54.6 1.2 fusion.194
  56.1 0.8 fusion.160
  56.9 0.6 constant_dynamic-update-slice_fusion
  57.5 1.2 convolution_add_fusion.7
  58.8 1.8 multiply_reduce_fusion
  61.0 0.9 copy-done.3
  62.8 1.3 collective-permute-start.4
  64.1 4.3 %collective-permute-start.7 = (bf16[1,16,256]{2,1,0:T(8,128)(2,1)S(1)}, bf16[1,16,256]{2,1,0:T(8,128)(2,1)S(1)}, u32[]{:S(2)}, u32[]{:S(2)}) collective-permute-start(bf16[1,16,256]{2,1,0:T(8,128)(2,1)S(1)} %slice.240), channel_id=1, source_target_pairs={{0,8},{8,16},{16,24},{1,9},{9,17},{17,25},{2,10},{10,18},{18,26},{... | collective-permute-start | bytes 24584 | tf_op jit(solution)/shard_map/ppermute | solution.py:15
  69.3 0.8 multiply_reduce_fusion.1
  71.1 1.3 collective-permute-start.5
  73.0 2.5 %collective-permute-done.5 = bf16[1,4,256]{2,1,0:T(4,128)(2,1)S(1)} collective-permute-done((bf16[1,4,256]{2,1,0:T(4,128)(2,1)S(1)}, bf16[1,4,256]{2,1,0:T(4,128)(2,1)S(1)}, u32[]{:S(2)}, u32[]{:S(2)}) %collective-permute-start.5) | collective-permute-done | bytes 2080 | tf_op jit(solution)/shard_map/ppermute | solution.py:15
  75.7 0.8 multiply_reduce_fusion.2
  77.5 1.5 collective-permute-start.6
  80.2 2.1 pad_maximum_fusion
  82.4 1.2 convolution_add_fusion.1
  83.6 1.7 fusion.29
  85.3 44.3 %all-reduce = (f32[4,256]{1,0:T(4,128)S(1)}, f32[4,256]{1,0:T(4,128)S(1)}) all-reduce(f32[4,256]{1,0:T(4,128)S(1)} %pad_maximum_fusion.8, f32[4,256]{1,0:T(4,128)S(1)} %pad_maximum_fusion.9), channel_id=1, replica_groups=mesh['seq'=4,'user'=8] {'seq','user'}, use_global_device_ids=true, to_apply=%region_21.0 | all-reduce | flops 2048 | bytes 16384 | tf_op jit(solution)/shard_map/psum | solution.py:115
  129.6 0.6 broadcast_multiply_fusion.2
  130.2 0.6 broadcast_multiply_fusion.1
  130.8 1.0 fusion.28
  131.8 93.8 %all-reduce.3.cloned.1.call-done = f32[4,3,256,256]{3,2,1,0:T(8,128)} async-done(((f32[4,3,256,256]{3,2,1,0:T(8,128)}), f32[4,3,256,256]{3,2,1,0:T(8,128)}) %all-reduce.3.cloned.1.call-update) | async-done | bytes 3145744 | tf_op jit(solution)/shard_map/psum | solution.py:115
  225.6 3.8 %broadcast_multiply_fusion = f32[4,3,256,256]{3,2,1,0:T(8,128)} fusion(f32[4,3,256,256]{3,2,1,0:T(8,128)} %all-reduce.3.cloned.1.call-done), kind=kLoop, calls=%fused_computation.3 | loop fusion | flops 786432 | bytes 6291456 | tf_op jit(solution)/shard_map/mul | solution.py:135
  (83 shorter events, 8.4 us)
Async XLA Ops:
  7.2 21.8 %copy-start = (bf16[1,16,128]{2,1,0:T(8,128)(2,1)S(1)}, bf16[1,16,128]{2,1,0:T(8,128)(2,1)}, u32[]{:S(2)}) copy-start(bf16[1,16,128]{2,1,0:T(8,128)(2,1)} %param.13) | copy-start | bytes 12292
  7.2 19.4 %copy-start.2 = (bf16[1,512,256]{2,1,0:T(8,128)(2,1)S(1)}, bf16[1,512,256]{2,1,0:T(8,128)(2,1)}, u32[]{:S(2)}) copy-start(bf16[1,512,256]{2,1,0:T(8,128)(2,1)} %param.9) | copy-start | bytes 786436
  7.2 19.4 %copy-start.4 = (f32[4,256]{1,0:T(4,128)S(1)}, f32[4,256]{1,0:T(4,128)}, u32[]{:S(2)}) copy-start(f32[4,256]{1,0:T(4,128)} %param.12) | copy-start | bytes 12292
  11.6 25.5 %collective-permute-start = (bf16[1,2,256]{2,1,0:T(2,128)(2,1)S(1)}, bf16[1,2,256]{2,1,0:T(2,128)(2,1)S(1)}, u32[]{:S(2)}, u32[]{:S(2)}) collective-permute-start(bf16[1,2,256]{2,1,0:T(2,128)(2,1)S(1)} %slice.220), channel_id=1, source_target_pairs={{0,8},{8,16},{16,24},{1,9},{9,17},{17,25},{2,10},{10,18},{18,26},{... | collective-permute-start | bytes 3080 | tf_op jit(solution)/shard_map/ppermute | solution.py:15
  14.7 42.2 %collective-permute-start.3 = (bf16[1,16,256]{2,1,0:T(8,128)(2,1)S(1)}, bf16[1,16,256]{2,1,0:T(8,128)(2,1)S(1)}, u32[]{:S(2)}, u32[]{:S(2)}) collective-permute-start(bf16[1,16,256]{2,1,0:T(8,128)(2,1)S(1)} %slice.198), channel_id=1, source_target_pairs={{8,0},{16,8},{24,16},{9,1},{17,9},{25,17},{10,2},{18,10},{26,18},{... | collective-permute-start | bytes 24584 | tf_op jit(solution)/shard_map/ppermute | solution.py:15
  19.9 13.0 %all-to-all-start = ((s32[1,8,2]{2,0,1:T(1,128)}), s32[1,8,2]{2,0,1:T(1,128)S(1)}, u32[]{:S(2)}, u32[]{:S(2)}) async-start(s32[1,8,2]{2,0,1:T(1,128)} %bitcast.75), calls=%async_computation | async-start | bytes 8192 | tf_op jit(solution)/shard_map/all_to_all | solution.py:130
  27.8 10.5 %copy-start.1 = (bf16[1,512,256]{2,1,0:T(8,128)(2,1)S(1)}, bf16[1,512,256]{2,1,0:T(8,128)(2,1)}, u32[]{:S(2)}) copy-start(bf16[1,512,256]{2,1,0:T(8,128)(2,1)} %param.8) | copy-start | bytes 786436
  33.0 23.1 %all-to-all-start.1 = ((bf16[1,8,2,128]{3,2,0,1:T(2,128)(2,1)}), bf16[1,8,2,128]{3,2,0,1:T(2,128)(2,1)S(1)}, u32[]{:S(2)}, u32[]{:S(2)}) async-start(bf16[1,8,2,128]{3,2,0,1:T(2,128)(2,1)} %fusion.162), calls=%async_computation.1 | async-start | bytes 8192 | tf_op jit(solution)/shard_map/all_to_all | solution.py:129
  37.0 188.6 %all-reduce.3.cloned.1.call-start = ((), (), s32[]{:S(2)}) async-start(), calls=%async_computation.2 | async-start | bytes 6291456 | tf_op jit(solution)/shard_map/psum | solution.py:115
  40.1 4.6 %collective-permute-start.1 = (bf16[1,4,256]{2,1,0:T(4,128)(2,1)S(1)}, bf16[1,4,256]{2,1,0:T(4,128)(2,1)S(1)}, u32[]{:S(2)}, u32[]{:S(2)}) collective-permute-start(bf16[1,4,256]{2,1,0:T(4,128)(2,1)S(1)} %slice.223), channel_id=1, source_target_pairs={{0,8},{8,16},{16,24},{1,9},{9,17},{17,25},{2,10},{10,18},{18,26},{... | collective-permute-start | bytes 6152 | tf_op jit(solution)/shard_map/ppermute | solution.py:15
  47.8 5.6 %collective-permute-start.2 = (bf16[1,8,256]{2,1,0:T(8,128)(2,1)S(1)}, bf16[1,8,256]{2,1,0:T(8,128)(2,1)S(1)}, u32[]{:S(2)}, u32[]{:S(2)}) collective-permute-start(bf16[1,8,256]{2,1,0:T(8,128)(2,1)S(1)} %slice.226), channel_id=1, source_target_pairs={{0,8},{8,16},{16,24},{1,9},{9,17},{17,25},{2,10},{10,18},{18,26},{... | collective-permute-start | bytes 12296 | tf_op jit(solution)/shard_map/ppermute | solution.py:15
  60.5 1.4 copy-start.3
  62.8 6.3 %collective-permute-start.4 = (bf16[1,8,256]{2,1,0:T(8,128)(2,1)S(1)}, bf16[1,8,256]{2,1,0:T(8,128)(2,1)S(1)}, u32[]{:S(2)}, u32[]{:S(2)}) collective-permute-start(bf16[1,8,256]{2,1,0:T(8,128)(2,1)S(1)} %slice.231), channel_id=1, source_target_pairs={{8,0},{16,8},{24,16},{9,1},{17,9},{25,17},{10,2},{18,10},{26,18},{... | collective-permute-start | bytes 12296 | tf_op jit(solution)/shard_map/ppermute | solution.py:15
  64.1 15.5 %collective-permute-start.7 = (bf16[1,16,256]{2,1,0:T(8,128)(2,1)S(1)}, bf16[1,16,256]{2,1,0:T(8,128)(2,1)S(1)}, u32[]{:S(2)}, u32[]{:S(2)}) collective-permute-start(bf16[1,16,256]{2,1,0:T(8,128)(2,1)S(1)} %slice.240), channel_id=1, source_target_pairs={{0,8},{8,16},{16,24},{1,9},{9,17},{17,25},{2,10},{10,18},{18,26},{... | collective-permute-start | bytes 24584 | tf_op jit(solution)/shard_map/ppermute | solution.py:15
  71.1 4.4 %collective-permute-start.5 = (bf16[1,4,256]{2,1,0:T(4,128)(2,1)S(1)}, bf16[1,4,256]{2,1,0:T(4,128)(2,1)S(1)}, u32[]{:S(2)}, u32[]{:S(2)}) collective-permute-start(bf16[1,4,256]{2,1,0:T(4,128)(2,1)S(1)} %slice.234), channel_id=1, source_target_pairs={{8,0},{16,8},{24,16},{9,1},{17,9},{25,17},{10,2},{18,10},{26,18},{... | collective-permute-start | bytes 6152 | tf_op jit(solution)/shard_map/ppermute | solution.py:15
  77.5 4.9 %collective-permute-start.6 = (bf16[1,2,256]{2,1,0:T(2,128)(2,1)S(1)}, bf16[1,2,256]{2,1,0:T(2,128)(2,1)S(1)}, u32[]{:S(2)}, u32[]{:S(2)}) collective-permute-start(bf16[1,2,256]{2,1,0:T(2,128)(2,1)S(1)} %slice.237), channel_id=1, source_target_pairs={{8,0},{16,8},{24,16},{9,1},{17,9},{25,17},{10,2},{18,10},{26,18},{... | collective-permute-start | bytes 3080 | tf_op jit(solution)/shard_map/ppermute | solution.py:15
Sparse Core Ops, SparseCore 0:
  82.4 143.1 all-reduce.2
where the time goes:
time: 237 us; the launch traced here: 236 us
  waiting for transfers between devices  98.4 us (42%)
  blocking collectives  44.3 us (19%)
  starting transfers between devices  30.8 us (13%)
  matrix products  24.5 us (10%)
  other arithmetic  17.1 us (7%)
  between operations  14.6 us (6%)
  local copies, waits for them, and re-layouts  6.56 us (3%)
    psum x1, waiting for transfers between devices, body(): lax.psum((weight_local, gain_local, bias_local), ('seq', 'user'))  93.8 us
    psum x1, blocking collectives, body(): lax.psum((weight_local, gain_local, bias_local), ('seq', 'user'))  44.3 us
    ppermute x8, starting transfers between devices, passed_along(): return lax.ppermute(block, axis, route)  20.1 us
    dot_general x9, matrix products, dilated(): jnp.dot(window, kernel[tap_index], preferred_element_type=jnp.float32)  10.6 us
    dot_general x12, matrix products, body(): lax.dot_general(window, weights[layer_num, tap_index], (((1,), (1,)), (()...  9.9 us
    all_to_all x1, starting transfers between devices, body(): lax.all_to_all(send_ids, 'user', split_axis=1, concat_axis=0, tiled=True)  6.62 us
  transfers between devices with their start and end apart: 11, of which 4 were waited for; matrix products, arithmetic and copies ran while one was open for 14% of the time, Pallas kernels for 0%

commit v1 on v0

--- a/solution.py
+++ b/solution.py
@@ -7,6 +7,10 @@
 TAPS = 3
 LAYERS = 4
 epsilon = 1e-05
+
+
+def launch_array_by_axis(mesh_dim, my_tile, across="user"):
+    return lax.psum(lax.psum(my_tile, across), mesh_dim)
 
 
 def passed_along(block, axis, distance):
@@ -112,8 +116,8 @@
     weight_local = jnp.stack(weight_terms)
     gain_local = jnp.stack(gain_terms)
     bias_local = jnp.stack(bias_terms)
-    weight_total, gain_total, bias_total = lax.psum(
-        (weight_local, gain_local, bias_local), ("seq", "user")
+    weight_total, gain_total, bias_total = launch_array_by_axis(
+        "seq", (weight_local, gain_local, bias_local)
     )
     factor = 1.0 / math.sqrt(user_count * lax.axis_size("user") * length * lax.axis_size("seq"))
     listing = jnp.argsort(table_owner, stable=True)

time: 237 us -> 266 us (1.12)
  waiting for transfers between devices: 98.4 us -> 160 us
  blocking collectives: 44.3 us -> 26.4 us
  matrix products: 24.5 us -> 12.6 us
    psum x1 -> x2, waiting for transfers between devices: 93.8 us -> 144 us  [launch_array_by_axis(): return lax.psum(lax.psum(my_tile, across), mesh_dim)]
    psum x1 -> x2, blocking collectives: 44.3 us -> 26.4 us  [launch_array_by_axis(): return lax.psum(lax.psum(my_tile, across), mesh_dim)]
    dot_general x9, matrix products: 10.6 us -> 2.42 us  [dilated(): jnp.dot(window, kernel[tap_index], preferred_element_type=jnp.float32)]
    all_to_all x1, waiting for transfers between devices: 0.01 us -> 6.44 us  [body(): lax.all_to_all(send_rows, 'user', split_axis=1, concat_axis=0, tiled=True)]
    dot_general x12, matrix products: 9.9 us -> 6.21 us  [body(): lax.dot_general(window, weights[layer_num, tap_index], (((1,), (1,)), (()...]
    all_to_all x1, waiting for transfers between devices: 1.96 us -> 5.31 us  [body(): lax.all_to_all(send_ids, 'user', split_axis=1, concat_axis=0, tiled=True)]
  transfers between devices with their start and end apart: 11 -> 12, of which waited for: 4 -> 7; matrix products, arithmetic and copies ran while one was open for 14% -> 8% of each run, Pallas kernels for 0% -> 0%
where the time goes in v1:
time: 266 us; the launch traced here: 265 us
  waiting for transfers between devices  160 us (60%)
  starting transfers between devices  30.2 us (11%)
  blocking collectives  26.4 us (10%)
  other arithmetic  16.5 us (6%)
  between operations  14.7 us (6%)
  matrix products  12.6 us (5%)
  local copies, waits for them, and re-layouts  5.57 us (2%)
    psum x2, waiting for transfers between devices, launch_array_by_axis(): return lax.psum(lax.psum(my_tile, across), mesh_dim)  144 us
    psum x2, blocking collectives, launch_array_by_axis(): return lax.psum(lax.psum(my_tile, across), mesh_dim)  26.4 us
    ppermute x8, starting transfers between devices, passed_along(): return lax.ppermute(block, axis, route)  21 us
    all_to_all x1, waiting for transfers between devices, body(): lax.all_to_all(send_rows, 'user', split_axis=1, concat_axis=0, tiled=True)  6.44 us
    dot_general x12, matrix products, body(): lax.dot_general(window, weights[layer_num, tap_index], (((1,), (1,)), (()...  6.21 us
    all_to_all x1, starting transfers between devices, body(): lax.all_to_all(send_ids, 'user', split_axis=1, concat_axis=0, tiled=True)  5.81 us
  transfers between devices with their start and end apart: 12, of which 7 were waited for; matrix products, arithmetic and copies ran while one was open for 8% of the time, Pallas kernels for 0%

profile of v1, /device:TPU:0, one launch (start us, length us, event | category | flops | bytes accessed | tf_op | source)
XLA Modules:
  0.0 265.4 jit_solution(15766958914851045870)
XLA Ops:
  7.2 0.9 fusion.190
  8.1 1.1 convert_reduce_fusion
  9.2 1.2 fusion.30
  10.4 1.3 fusion.21
  11.7 2.4 collective-permute-start
  14.1 0.7 slice.198
  14.8 1.3 collective-permute-start.3
  16.1 0.8 fusion.191
  16.9 1.2 fusion.104
  18.7 0.4 copy-done.2
  19.1 0.3 fusion.192
  20.0 5.2 %collective-permute-start.1 = (bf16[1,4,256]{2,1,0:T(4,128)(2,1)S(1)}, bf16[1,4,256]{2,1,0:T(4,128)(2,1)S(1)}, u32[]{:S(2)}, u32[]{:S(2)}) collective-permute-start(bf16[1,4,256]{2,1,0:T(4,128)(2,1)S(1)} %slice.223), channel_id=1, source_target_pairs={{0,8},{8,16},{16,24},{1,9},{9,17},{17,25},{2,10},{10,18},{18,26},{... | collective-permute-start | bytes 6152 | tf_op jit(solution)/shard_map/ppermute | solution.py:19
  25.4 0.6 collective-permute-done.1
  26.2 0.4 fusion.193
  27.2 3.5 %collective-permute-start.2 = (bf16[1,8,256]{2,1,0:T(8,128)(2,1)S(1)}, bf16[1,8,256]{2,1,0:T(8,128)(2,1)S(1)}, u32[]{:S(2)}, u32[]{:S(2)}) collective-permute-start(bf16[1,8,256]{2,1,0:T(8,128)(2,1)S(1)} %slice.226), channel_id=1, source_target_pairs={{0,8},{8,16},{16,24},{1,9},{9,17},{17,25},{2,10},{10,18},{18,26},{... | collective-permute-start | bytes 12296 | tf_op jit(solution)/shard_map/ppermute | solution.py:19
  31.0 0.6 collective-permute-done.2
  32.7 0.8 multiply_reduce_fusion
  33.4 0.5 fusion.189
  34.8 1.3 collective-permute-start.4
  36.1 4.7 %collective-permute-start.7 = (bf16[1,16,256]{2,1,0:T(8,128)(2,1)S(1)}, bf16[1,16,256]{2,1,0:T(8,128)(2,1)S(1)}, u32[]{:S(2)}, u32[]{:S(2)}) collective-permute-start(bf16[1,16,256]{2,1,0:T(8,128)(2,1)S(1)} %slice.240), channel_id=1, source_target_pairs={{0,8},{8,16},{16,24},{1,9},{9,17},{17,25},{2,10},{10,18},{18,26},{... | collective-permute-start | bytes 24584 | tf_op jit(solution)/shard_map/ppermute | solution.py:19
  41.7 0.8 multiply_reduce_fusion.1
  42.5 0.4 fusion.188
  43.5 1.3 collective-permute-start.5
  45.4 2.9 %collective-permute-done.5 = bf16[1,4,256]{2,1,0:T(4,128)(2,1)S(1)} collective-permute-done((bf16[1,4,256]{2,1,0:T(4,128)(2,1)S(1)}, bf16[1,4,256]{2,1,0:T(4,128)(2,1)S(1)}, u32[]{:S(2)}, u32[]{:S(2)}) %collective-permute-start.5) | collective-permute-done | bytes 2080 | tf_op jit(solution)/shard_map/ppermute | solution.py:19
  48.6 0.8 multiply_reduce_fusion.2
  49.4 0.4 fusion.187
  51.3 2.1 pad_maximum_fusion
  53.4 0.6 copy-done.5
  54.0 1.2 sort.17
  55.2 0.7 gather_fusion
  55.9 0.7 reshape.430
  56.6 5.8 %all-to-all-start = ((s32[1,8,2]{2,0,1:T(1,128)}), s32[1,8,2]{2,0,1:T(1,128)S(1)}, u32[]{:S(2)}, u32[]{:S(2)}) async-start(s32[1,8,2]{2,0,1:T(1,128)} %bitcast.75), calls=%async_computation | async-start | bytes 8192 | tf_op jit(solution)/shard_map/all_to_all | solution.py:134
  62.4 0.6 gather_fusion.1
  63.1 0.7 fusion.162
  63.7 5.3 %all-to-all-done = s32[1,8,2]{2,0,1:T(1,128)S(1)} async-done(((s32[1,8,2]{2,0,1:T(1,128)}), s32[1,8,2]{2,0,1:T(1,128)S(1)}, u32[]{:S(2)}, u32[]{:S(2)}) %all-to-all-start) | async-done | bytes 96 | tf_op jit(solution)/shard_map/all_to_all | solution.py:134
  69.1 3.3 %all-to-all-start.1 = ((bf16[1,8,2,128]{3,2,0,1:T(2,128)(2,1)}), bf16[1,8,2,128]{3,2,0,1:T(2,128)(2,1)S(1)}, u32[]{:S(2)}, u32[]{:S(2)}) async-start(bf16[1,8,2,128]{3,2,0,1:T(2,128)(2,1)} %fusion.162), calls=%async_computation.1 | async-start | bytes 8192 | tf_op jit(solution)/shard_map/all_to_all | solution.py:133
  72.5 6.4 %all-to-all-done.1 = bf16[1,8,2,128]{3,2,0,1:T(2,128)(2,1)S(1)} async-done(((bf16[1,8,2,128]{3,2,0,1:T(2,128)(2,1)}), bf16[1,8,2,128]{3,2,0,1:T(2,128)(2,1)S(1)}, u32[]{:S(2)}, u32[]{:S(2)}) %all-to-all-start.1) | async-done | bytes 4128 | tf_op jit(solution)/shard_map/all_to_all | solution.py:133
  79.0 0.8 fusion.160
  79.7 1.3 collective-permute-start.6
  81.3 103.3 %all-reduce.5.cloned.1.call-done = f32[4,3,256,256]{3,2,1,0:T(8,128)} async-done(((f32[4,3,256,256]{3,2,1,0:T(8,128)}), f32[4,3,256,256]{3,2,1,0:T(8,128)}) %all-reduce.5.cloned.1.call-update) | async-done | bytes 3145744 | tf_op jit(solution)/shard_map/psum | solution.py:13
  185.0 0.8 fusion.29
  185.8 19.7 %all-reduce = (f32[4,256]{1,0:T(4,128)S(1)}, f32[4,256]{1,0:T(4,128)S(1)}) all-reduce(f32[4,256]{1,0:T(4,128)S(1)} %pad_maximum_fusion.8, f32[4,256]{1,0:T(4,128)S(1)} %pad_maximum_fusion.9), channel_id=1, replica_groups=mesh['seq'=4,'user'=8] {'user'}, use_global_device_ids=true, to_apply=%region_22.0 | all-reduce | flops 2048 | bytes 16384 | tf_op jit(solution)/shard_map/psum | solution.py:13
  205.4 6.8 %all-reduce.1 = (f32[4,256]{1,0:T(4,128)S(1)}, f32[4,256]{1,0:T(4,128)S(1)}) all-reduce(f32[4,256]{1,0:T(4,128)S(1)} %get-tuple-element.19, f32[4,256]{1,0:T(4,128)S(1)} %get-tuple-element.20), channel_id=1, replica_groups=mesh['seq'=4,'user'=8] {'seq'}, use_global_device_ids=true, to_apply=%region_23.0 | all-reduce | flops 2048 | bytes 16384 | tf_op jit(solution)/shard_map/psum | solution.py:13
  212.2 0.6 broadcast_multiply_fusion.2
  212.8 0.6 broadcast_multiply_fusion.1
  213.4 1.0 fusion.28
  214.5 40.3 %all-reduce.7.cloned.1.call-done = f32[4,3,256,256]{3,2,1,0:T(8,128)} async-done(((f32[4,3,256,256]{3,2,1,0:T(8,128)}), f32[4,3,256,256]{3,2,1,0:T(8,128)}) %all-reduce.7.cloned.1.call-update) | async-done | bytes 3145744 | tf_op jit(solution)/shard_map/psum | solution.py:13
  254.8 3.8 %broadcast_multiply_fusion = f32[4,3,256,256]{3,2,1,0:T(8,128)} fusion(f32[4,3,256,256]{3,2,1,0:T(8,128)} %all-reduce.7.cloned.1.call-done), kind=kLoop, calls=%fused_computation.3 | loop fusion | flops 786432 | bytes 6291456 | tf_op jit(solution)/shard_map/mul | solution.py:139
  (89 shorter events, 8.8 us)
Async XLA Ops:
  7.2 55.2 %copy-start = (bf16[1,16,128]{2,1,0:T(8,128)(2,1)S(1)}, bf16[1,16,128]{2,1,0:T(8,128)(2,1)}, u32[]{:S(2)}) copy-start(bf16[1,16,128]{2,1,0:T(8,128)(2,1)} %param.13) | copy-start | bytes 12292
  7.2 11.2 %copy-start.3 = (bf16[1,512,256]{2,1,0:T(8,128)(2,1)S(1)}, bf16[1,512,256]{2,1,0:T(8,128)(2,1)}, u32[]{:S(2)}) copy-start(bf16[1,512,256]{2,1,0:T(8,128)(2,1)} %param.9) | copy-start | bytes 786436
  7.2 11.0 %copy-start.4 = (bf16[4,3,256,256]{3,2,1,0:T(8,128)(2,1)S(1)}, bf16[4,3,256,256]{3,2,1,0:T(8,128)(2,1)}, u32[]{:S(2)}) copy-start(bf16[4,3,256,256]{3,2,1,0:T(8,128)(2,1)} %param.10) | copy-start | bytes 4718596
  7.2 177.4 %all-reduce.5.cloned.1.call-start = ((), (), s32[]{:S(2)}) async-start(), calls=%async_computation.2 | async-start | bytes 6291456 | tf_op jit(solution)/shard_map/psum | solution.py:13
  11.7 6.7 %collective-permute-start = (bf16[1,2,256]{2,1,0:T(2,128)(2,1)S(1)}, bf16[1,2,256]{2,1,0:T(2,128)(2,1)S(1)}, u32[]{:S(2)}, u32[]{:S(2)}) collective-permute-start(bf16[1,2,256]{2,1,0:T(2,128)(2,1)S(1)} %slice.220), channel_id=1, source_target_pairs={{0,8},{8,16},{16,24},{1,9},{9,17},{17,25},{2,10},{10,18},{18,26},{... | collective-permute-start | bytes 3080 | tf_op jit(solution)/shard_map/ppermute | solution.py:19
  14.8 17.6 %collective-permute-start.3 = (bf16[1,16,256]{2,1,0:T(8,128)(2,1)S(1)}, bf16[1,16,256]{2,1,0:T(8,128)(2,1)S(1)}, u32[]{:S(2)}, u32[]{:S(2)}) collective-permute-start(bf16[1,16,256]{2,1,0:T(8,128)(2,1)S(1)} %slice.198), channel_id=1, source_target_pairs={{8,0},{16,8},{24,16},{9,1},{17,9},{25,17},{10,2},{18,10},{26,18},{... | collective-permute-start | bytes 24584 | tf_op jit(solution)/shard_map/ppermute | solution.py:19
  18.1 1.0 copy-start.2
  20.0 6.0 %collective-permute-start.1 = (bf16[1,4,256]{2,1,0:T(4,128)(2,1)S(1)}, bf16[1,4,256]{2,1,0:T(4,128)(2,1)S(1)}, u32[]{:S(2)}, u32[]{:S(2)}) collective-permute-start(bf16[1,4,256]{2,1,0:T(4,128)(2,1)S(1)} %slice.223), channel_id=1, source_target_pairs={{0,8},{8,16},{16,24},{1,9},{9,17},{17,25},{2,10},{10,18},{18,26},{... | collective-permute-start | bytes 6152 | tf_op jit(solution)/shard_map/ppermute | solution.py:19
  27.2 4.4 %collective-permute-start.2 = (bf16[1,8,256]{2,1,0:T(8,128)(2,1)S(1)}, bf16[1,8,256]{2,1,0:T(8,128)(2,1)S(1)}, u32[]{:S(2)}, u32[]{:S(2)}) collective-permute-start(bf16[1,8,256]{2,1,0:T(8,128)(2,1)S(1)} %slice.226), channel_id=1, source_target_pairs={{0,8},{8,16},{16,24},{1,9},{9,17},{17,25},{2,10},{10,18},{18,26},{... | collective-permute-start | bytes 12296 | tf_op jit(solution)/shard_map/ppermute | solution.py:19
  34.8 6.7 %collective-permute-start.4 = (bf16[1,8,256]{2,1,0:T(8,128)(2,1)S(1)}, bf16[1,8,256]{2,1,0:T(8,128)(2,1)S(1)}, u32[]{:S(2)}, u32[]{:S(2)}) collective-permute-start(bf16[1,8,256]{2,1,0:T(8,128)(2,1)S(1)} %slice.231), channel_id=1, source_target_pairs={{8,0},{16,8},{24,16},{9,1},{17,9},{25,17},{10,2},{18,10},{26,18},{... | collective-permute-start | bytes 12296 | tf_op jit(solution)/shard_map/ppermute | solution.py:19
  36.1 14.6 %collective-permute-start.7 = (bf16[1,16,256]{2,1,0:T(8,128)(2,1)S(1)}, bf16[1,16,256]{2,1,0:T(8,128)(2,1)S(1)}, u32[]{:S(2)}, u32[]{:S(2)}) collective-permute-start(bf16[1,16,256]{2,1,0:T(8,128)(2,1)S(1)} %slice.240), channel_id=1, source_target_pairs={{0,8},{8,16},{16,24},{1,9},{9,17},{17,25},{2,10},{10,18},{18,26},{... | collective-permute-start | bytes 24584 | tf_op jit(solution)/shard_map/ppermute | solution.py:19
  43.5 4.8 %collective-permute-start.5 = (bf16[1,4,256]{2,1,0:T(4,128)(2,1)S(1)}, bf16[1,4,256]{2,1,0:T(4,128)(2,1)S(1)}, u32[]{:S(2)}, u32[]{:S(2)}) collective-permute-start(bf16[1,4,256]{2,1,0:T(4,128)(2,1)S(1)} %slice.234), channel_id=1, source_target_pairs={{8,0},{16,8},{24,16},{9,1},{17,9},{25,17},{10,2},{18,10},{26,18},{... | collective-permute-start | bytes 6152 | tf_op jit(solution)/shard_map/ppermute | solution.py:19
  53.3 0.7 copy-start.5
  53.3 1.9 copy-start.1
  56.6 12.5 %all-to-all-start = ((s32[1,8,2]{2,0,1:T(1,128)}), s32[1,8,2]{2,0,1:T(1,128)S(1)}, u32[]{:S(2)}, u32[]{:S(2)}) async-start(s32[1,8,2]{2,0,1:T(1,128)} %bitcast.75), calls=%async_computation | async-start | bytes 8192 | tf_op jit(solution)/shard_map/all_to_all | solution.py:134
  69.1 9.9 %all-to-all-start.1 = ((bf16[1,8,2,128]{3,2,0,1:T(2,128)(2,1)}), bf16[1,8,2,128]{3,2,0,1:T(2,128)(2,1)S(1)}, u32[]{:S(2)}, u32[]{:S(2)}) async-start(bf16[1,8,2,128]{3,2,0,1:T(2,128)(2,1)} %fusion.162), calls=%async_computation.1 | async-start | bytes 8192 | tf_op jit(solution)/shard_map/all_to_all | solution.py:133
  72.4 182.4 %all-reduce.7.cloned.1.call-start = ((), (), s32[]{:S(2)}) async-start(), calls=%async_computation.3 | async-start | bytes 6291456 | tf_op jit(solution)/shard_map/psum | solution.py:13
  79.7 104.9 %collective-permute-start.6 = (bf16[1,2,256]{2,1,0:T(2,128)(2,1)S(1)}, bf16[1,2,256]{2,1,0:T(2,128)(2,1)S(1)}, u32[]{:S(2)}, u32[]{:S(2)}) collective-permute-start(bf16[1,2,256]{2,1,0:T(2,128)(2,1)S(1)} %slice.237), channel_id=1, source_target_pairs={{8,0},{16,8},{24,16},{9,1},{17,9},{25,17},{10,2},{18,10},{26,18},{... | collective-permute-start | bytes 3080 | tf_op jit(solution)/shard_map/ppermute | solution.py:19
Sparse Core Ops, SparseCore 0:
  53.5 131.1 all-reduce.4
  187.0 67.7 all-reduce.6
